TPU v7x, 32 devices: a whole 2x2x4 slice. The times are simulated.
32 devices in a mesh: sec: 2 (over core), dp: 4 (over y, x), mp: 4 (over z).
Axes of the slice: x: 2, y: 2, z: 4, core: 2. Of those that a mesh axis runs over, the one named last changes fastest.
Arguments:
- section_rows: bfloat16 [2, 512, 4096], P('sec', 'dp'), may hold values from -6 to 6
- proj_weights: bfloat16 [2, 4096, 8, 128], P('sec', None, 'mp'), may hold values from -1 to 1
- out_grad: bfloat16 [512, 4096], P('dp'), may hold values from -6 to 6
- ffn_gain: float32 [4096], replicated, may hold values from 0.5 to 1.5
- ffn_in: bfloat16 [4096, 2, 1536], P(None, None, ('sec', 'mp')), may hold values from -0.09375 to 0.09375
- ffn_out: bfloat16 [1536, 4096], P(('sec', 'mp')), may hold values from -0.15625 to 0.15625
- grow_level: int32 [1536], P(('sec', 'mp')), may hold values from 0 to 4, as said below
- dec_seg: int32 [4, 128], P('dp'), may hold values from 0 to 1, never falling along the last dimension, each value on 1 to 96 neighbouring positions
- enc_seg: int32 [4, 128], P('dp'), may hold values from 0 to 1, never falling along the last dimension, each value on 1 to 96 neighbouring positions
Outputs:
- layer_out: bfloat16 [512, 4096], P('dp', ('sec', 'mp'))
- proj_grads: bfloat16 [2, 4096, 8, 128], P('sec', 'dp', 'mp')
Inputs may be any that keep to these rules, and one draw needn't show every extreme that they name: `grow_level`: units below 1024 have level 4. `dec_seg`: each of the 2 examples has entries in every group. `enc_seg`: each of the 2 examples has entries in every group.
All inputs are finite; a program needn't handle non-finite values.
Results may differ from a plain program's by a relative error of at most 0.025.
Values may be sent and summed in bfloat16 or wider, within the bound.
A program may use at most 64 MiB of HBM per device.

v0:
```python
import functools

import jax
import jax.numpy as jnp
from jax import lax
from jax.experimental import pallas as pl
from jax.experimental.pallas import tpu as pltpu
from jax.sharding import PartitionSpec as P

norm_eps = 1e-06
pieces = 2
F32 = jnp.float32
BF16 = jnp.bfloat16


def contract(left, right, left_dim, right_dim):
    dims = (((left_dim,), (right_dim,)), ((), ()))
    return lax.dot_general(left, right, dims, preferred_element_type=F32)


def remote(src, dst, send, recv, device):
    return pltpu.make_async_remote_copy(
        src_ref=src,
        dst_ref=dst,
        send_sem=send,
        recv_sem=recv,
        device_id=device,
        device_id_type=pl.DeviceIdType.MESH,
    )


def body(
    n_dp,
    n_mp,
    rows_hbm,
    weight_hbm,
    grad_hbm,
    gain_hbm,
    ffn_in_hbm,
    ffn_out_hbm,
    level_hbm,
    dec_seg_hbm,
    enc_seg_hbm,
    layer_out,
    proj_grads,
    rows,
    weight,
    grad,
    gain,
    ffn_in,
    ffn_out,
    level,
    dec_seg,
    enc_seg,
    w_left,
    w_right,
    kv_send,
    kv_recv,
    wo_all,
    ctx_all,
    rows_all,
    grad_all,
    g_send,
    g_all,
    mix,
    part_send,
    part_recv,
    fold_send,
    fold_recv,
    t_left,
    t_right,
    rows_sem,
    grad_sem,
    g_sem,
    wo_sem,
    ctx_sem,
    mix_sem,
    fwd_sem,
    part_sem,
    fold_sem,
    kv_sem,
    gkv_sem,
    weight_sem,
    load_sem,
    slot_sem,
):
    sec = lax.axis_index("sec")
    dp = lax.axis_index("dp")
    mp = lax.axis_index("mp")
    n_rows, width = rows.shape
    lanes = weight.shape[1]
    half = lanes // 2
    block = width // n_mp
    share = width // (2 * n_mp)
    cut = width // n_dp
    units = ffn_out.shape[0]
    is_dec = sec == 1
    is_enc = sec == 0
    other = {"sec": 1 - sec}

    def dp_at(t):
        return lax.rem(dp + t, n_dp)

    def mp_at(t):
        return lax.rem(mp + t, n_mp)

    def mp_from(t):
        return lax.rem(mp + n_mp - t, n_mp)

    def cols(index, size):
        return pl.ds(pl.multiple_of(index * size, size), size)

    def weight_load(t):
        part = cols(mp_at(t), 2 * block)
        return pltpu.make_async_copy(
            weight_hbm.at[part, :], weight.at[part, :], weight_sem.at[t]
        )

    pairs = (
        (rows_hbm, rows),
        (grad_hbm, grad),
        (dec_seg_hbm, dec_seg),
        (enc_seg_hbm, enc_seg),
        (ffn_in_hbm, ffn_in),
        (gain_hbm, gain),
        (level_hbm, level),
        (ffn_out_hbm, ffn_out),
    )
    loads = [pltpu.make_async_copy(a, b, load_sem.at[i]) for i, (a, b) in enumerate(pairs)]
    own_rows = pltpu.make_async_copy(rows_hbm.at[:, cols(dp, cut)], rows_all.at[0], slot_sem.at[0])
    own_grad = pltpu.make_async_copy(grad_hbm.at[:, cols(dp, cut)], grad_all.at[0], slot_sem.at[1])
    for t in list(range(1, n_mp)) + [0]:
        weight_load(t).start()
    for load in loads:
        load.start()
    own_rows.start()
    own_grad.start()

    barrier = pltpu.get_barrier_semaphore()
    pl.semaphore_signal(barrier, inc=1, device_id=other, device_id_type=pl.DeviceIdType.MESH)
    for t in range(1, n_dp):
        pl.semaphore_signal(
            barrier, inc=1, device_id={"dp": dp_at(t)}, device_id_type=pl.DeviceIdType.MESH
        )
    for t in range(1, n_mp):
        pl.semaphore_signal(
            barrier, inc=1, device_id={"mp": mp_at(t)}, device_id_type=pl.DeviceIdType.MESH
        )
    pl.semaphore_wait(barrier, n_dp + n_mp - 1)

    def piece(c):
        return pl.ds(c * (n_rows // pieces), n_rows // pieces)

    def rows_copy(t):
        to = dp_at(t)
        return remote(
            rows_hbm.at[:, cols(to, cut)], rows_all.at[t], rows_sem.at[0, t], rows_sem.at[1, t], {"dp": to}
        )

    def grad_copy(t):
        to = dp_at(t)
        return remote(
            grad_hbm.at[:, cols(to, cut)], grad_all.at[t], grad_sem.at[0, t], grad_sem.at[1, t], {"dp": to}
        )

    def g_copy(t):
        return remote(
            g_all.at[0], g_all.at[t], g_sem.at[0, t], g_sem.at[1, t], {"dp": dp_at(t)}
        )

    def wo_copy(t):
        to = mp_at(t)
        return remote(
            w_right.at[cols(to, block), :],
            wo_all.at[t],
            wo_sem.at[0, t],
            wo_sem.at[1, t],
            {"mp": to},
        )

    def ctx_copy(t):
        return remote(
            ctx_all.at[0], ctx_all.at[t], ctx_sem.at[0, t], ctx_sem.at[1, t], {"mp": mp_at(t)}
        )

    def mix_copy(c, t):
        return remote(
            mix.at[0, piece(c), :],
            mix.at[t, piece(c), :],
            mix_sem.at[0, c, t],
            mix_sem.at[1, c, t],
            {"mp": mp_at(t)},
        )

    def fwd_copy(c, t):
        ref = mix.at[t, piece(c), :]
        return remote(ref, ref, fwd_sem.at[0, c, t], fwd_sem.at[1, c, t], other)

    def part_copy(c, t):
        return remote(
            part_send.at[t, piece(c), :],
            part_recv.at[t, piece(c), :],
            part_sem.at[0, c, t],
            part_sem.at[1, c, t],
            other,
        )

    def fold_copy(c, t):
        return remote(
            fold_send.at[t, piece(c), :],
            fold_recv.at[t, piece(c), :],
            fold_sem.at[0, c, t],
            fold_sem.at[1, c, t],
            {"mp": mp_at(t)},
        )

    kv_copy = remote(kv_send, kv_recv, kv_sem.at[0], kv_sem.at[1], other)
    gkv_copy = remote(g_send, g_all.at[0], gkv_sem.at[0], gkv_sem.at[1], other)

    for t in range(1, n_dp):
        rows_copy(t).start()

    @pl.when(is_dec)
    def _():
        for t in range(1, n_dp):
            grad_copy(t).start()

    tile = 2 * lanes
    out_id = lax.broadcasted_iota(jnp.int32, (tile, tile), 0)
    in_id = lax.broadcasted_iota(jnp.int32, (tile, tile), 1)
    wanted = jnp.where(out_id < lanes, 2 * out_id, 2 * (out_id - lanes) + 1)
    pick = jnp.where(in_id == wanted, 1.0, 0.0).astype(BF16)
    first = lax.broadcasted_iota(jnp.int32, (lanes, lanes), 1) < half

    for t in list(range(1, n_mp)) + [0]:
        begin = mp_at(t) * block
        weight_load(t).wait()
        for i in range(block // lanes):
            d = pl.multiple_of(begin + i * lanes, lanes)
            two = contract(pick, weight[pl.ds(pl.multiple_of(2 * d, tile), tile), :], 1, 0)
            one, second = two[:lanes], two[lanes:]
            w_left[pl.ds(d, lanes), :] = jnp.where(
                first, one, pltpu.roll(second, half, 1)
            ).astype(BF16)
            w_right[pl.ds(d, lanes), :] = jnp.where(
                first, pltpu.roll(one, half, 1), second
            ).astype(BF16)

        if t > 0:

            @pl.when(is_dec)
            def _():
                wo_copy(t).start()

    loads[0].wait()
    loads[1].wait()

    @pl.when(is_enc)
    def _():
        kv_send[0] = contract(rows[...], w_left[...], 1, 0).astype(BF16)
        kv_send[1] = contract(rows[...], w_right[...], 1, 0).astype(BF16)
        kv_copy.start()

    for load in loads[2:]:
        load.wait()

    @pl.when(is_dec)
    def _():
        wide_q = contract(rows[...], w_left[...], 1, 0)
        wide_gc = contract(grad[...], w_right[...], 1, 0)
        q = wide_q.astype(BF16)
        gc = wide_gc.astype(BF16)
        dec = jnp.transpose(jnp.broadcast_to(dec_seg[...].astype(F32), (n_rows, n_rows)))
        same = dec == jnp.broadcast_to(enc_seg[...].astype(F32), (n_rows, n_rows))
        kv_copy.wait_recv()
        key = kv_recv[0]
        value = kv_recv[1]
        probs, lows, contexts = [], [], []
        for h in range(2):
            mine = first if h == 0 else jnp.logical_not(first)
            scores = contract(jnp.where(mine, wide_q, 0.0).astype(BF16), key, 1, 1)
            scores = jnp.where(same, scores, -1e30)
            scores = jnp.exp(scores - jnp.max(scores, axis=1, keepdims=True))
            prob = scores / jnp.sum(scores, axis=1, keepdims=True)
            low = prob.astype(BF16)
            probs.append(prob)
            lows.append(low)
            contexts.append(contract(low, value, 1, 0))
        context = jnp.where(first, contexts[0], contexts[1]).astype(BF16)
        ctx_all[0] = context
        g_all[0, :, lanes:] = context
        for t in range(1, n_mp):
            ctx_copy(t).start()
        gqs, gks, gvs = [], [], []
        for h in range(2):
            mine = first if h == 0 else jnp.logical_not(first)
            grad_prob = contract(jnp.where(mine, wide_gc, 0.0).astype(BF16), value, 1, 1)
            total = jnp.sum(grad_prob * probs[h], axis=1, keepdims=True)
            score = (probs[h] * (grad_prob - total)).astype(BF16)
            gqs.append(contract(score, key, 1, 0))
            gks.append(contract(score, q, 0, 0))
            gvs.append(contract(lows[h], gc, 0, 0))
        g_send[:, :lanes] = jnp.where(first, gks[0], gks[1]).astype(BF16)
        g_send[:, lanes:] = jnp.where(first, gvs[0], gvs[1]).astype(BF16)
        gkv_copy.start()
        g_all[0, :, :lanes] = jnp.where(first, gqs[0], gqs[1]).astype(BF16)

    @pl.when(is_enc)
    def _():
        gkv_copy.wait_recv()

    for t in range(1, n_dp):
        g_copy(t).start()

    @pl.when(is_dec)
    def _():
        for t in range(1, n_mp):
            wo_copy(t).wait_recv()
            ctx_copy(t).wait_recv()
        for c in range(pieces):
            own = contract(ctx_all[0, piece(c), :], w_right[cols(mp, block), :], 1, 1)
            total = rows[piece(c), cols(mp, block)].astype(F32) + own
            for t in range(1, n_mp):
                total = total + contract(ctx_all[t, piece(c), :], wo_all[t], 1, 1)
            mix[0, piece(c), :] = total.astype(BF16)
            for t in range(1, n_mp):
                mix_copy(c, t).start()
            fwd_copy(c, 0).start()

    own_rows.wait()
    own_grad.wait()

    for t in range(1, n_dp):
        rows_copy(t).wait_recv()

        @pl.when(is_dec)
        def _():
            grad_copy(t).wait_recv()

        g_copy(t).wait_recv()
    flat_rows = rows_all[...].reshape(n_dp * n_rows, cut)
    g_flat = g_all[...].reshape(n_dp * n_rows, 2 * lanes)
    t_left[...] = contract(g_flat[:, :lanes], flat_rows, 0, 0).astype(BF16)

    @pl.when(is_enc)
    def _():
        t_right[...] = contract(g_flat[:, lanes:], flat_rows, 0, 0).astype(BF16)

    @pl.when(is_dec)
    def _():
        flat_grad = grad_all[...].reshape(n_dp * n_rows, cut)
        t_right[...] = contract(g_flat[:, lanes:], flat_grad, 0, 0).astype(BF16)

    row_id = lax.broadcasted_iota(jnp.int32, (tile, lanes), 0)
    d_id = lax.broadcasted_iota(jnp.int32, (tile, lanes), 1)
    spread = [jnp.where(row_id == 2 * d_id + h, 1.0, 0.0).astype(BF16) for h in range(2)]
    for i in range(cut // lanes):
        part = slice(i * lanes, (i + 1) * lanes)
        heads = [
            jnp.concatenate(
                [t_left[h * half : (h + 1) * half, part], t_right[h * half : (h + 1) * half, part]],
                axis=0,
            )
            for h in range(2)
        ]
        woven = contract(spread[0], heads[0], 1, 1) + contract(spread[1], heads[1], 1, 1)
        proj_grads[i * tile : (i + 1) * tile, :] = woven.astype(BF16)

    order = list(range(1, n_mp)) + [0]
    place = sec * n_mp + mp
    slot = lax.rem(mp + n_mp - place // 2, n_mp)
    kept = []
    for c in range(pieces):
        gate = jnp.zeros((n_rows // pieces, units), F32)
        up = jnp.zeros((n_rows // pieces, units), F32)
        square = jnp.zeros((n_rows // pieces, 1), F32)
        for t in range(n_mp):
            if t > 0:

                @pl.when(is_dec)
                def _():
                    mix_copy(c, t).wait_recv()
                    fwd_copy(c, t).start()

            @pl.when(is_enc)
            def _():
                fwd_copy(c, t).wait_recv()

            where = cols(mp_from(t), block)
            wide = mix[t, piece(c), :].astype(F32)
            square = square + jnp.sum(wide * wide, axis=1, keepdims=True)
            scaled = (wide * gain[:, where]).astype(BF16)
            gate = gate + contract(scaled, ffn_in[:units, where], 1, 1)
            up = up + contract(scaled, ffn_in[units:, where], 1, 1)
        inverse = lax.rsqrt(square / width + norm_eps)
        gate = gate * inverse
        up = up * inverse
        unit_level = level[...].astype(F32) * 0.25
        hidden = (jax.nn.gelu(gate, approximate=True) * up * unit_level).astype(BF16)
        for t in order:
            far = (1 - sec) * n_mp + mp_at(t)
            part_send[t, piece(c), :] = contract(
                hidden, ffn_out[:, cols(far, share)], 1, 0
            ).astype(BF16)
            part_copy(c, t).start()
        for t in order:
            near = sec * n_mp + mp_at(t)
            own = contract(hidden, ffn_out[:, cols(near, share)], 1, 0)
            part_copy(c, t).wait_recv()
            own = own + part_recv[t, piece(c), :].astype(F32)
            if t > 0:
                fold_send[t, piece(c), :] = own.astype(BF16)
                fold_copy(c, t).start()
            else:
                there = cols(lax.rem(place, 2), share)
                kept.append(own + mix[slot, piece(c), there].astype(F32))
    for c in range(pieces):
        mine = kept[c]
        for t in range(1, n_mp):
            fold_copy(c, t).wait_recv()
            mine = mine + fold_recv[t, piece(c), :].astype(F32)
        layer_out[piece(c), :] = mine.astype(BF16)

    for t in range(1, n_dp):
        rows_copy(t).wait_send()
        g_copy(t).wait_send()
    for c in range(pieces):
        for t in range(1, n_mp):
            fold_copy(c, t).wait_send()
        for t in range(n_mp):
            part_copy(c, t).wait_send()

    @pl.when(is_enc)
    def _():
        kv_copy.wait_send()

    @pl.when(is_dec)
    def _():
        gkv_copy.wait_send()
        for t in range(1, n_dp):
            grad_copy(t).wait_send()
        for t in range(1, n_mp):
            wo_copy(t).wait_send()
            ctx_copy(t).wait_send()
        for c in range(pieces):
            for t in range(1, n_mp):
                mix_copy(c, t).wait_send()
            for t in range(n_mp):
                fwd_copy(c, t).wait_send()


def hand_over(a, b, a_out, b_out):
    a_out[...] = a[...]
    b_out[...] = b[...]


def on_device(
    n_dp,
    n_mp,
    section_rows,
    proj_weights,
    out_grad,
    ffn_gain,
    ffn_in,
    ffn_out,
    grow_level,
    dec_seg,
    enc_seg,
):
    rows = section_rows[0]
    n_rows, width = rows.shape
    heads, lanes = proj_weights.shape[2:]
    weight = proj_weights.reshape(width * heads, lanes)
    units = ffn_out.shape[0]
    gates = jnp.transpose(ffn_in, (1, 2, 0)).reshape(2 * units, width)
    block, share, cut = width // n_mp, width // (2 * n_mp), width // n_dp
    vmem = pl.BlockSpec(memory_space=pltpu.VMEM)

    def sems(*shape):
        return pltpu.SemaphoreType.DMA(shape)

    operands = (
        rows,
        weight,
        out_grad,
        ffn_gain[None],
        gates,
        ffn_out,
        grow_level[None],
        dec_seg,
        enc_seg,
    )
    layer_out, grads = pl.pallas_call(
        functools.partial(body, n_dp, n_mp),
        out_shape=(
            jax.ShapeDtypeStruct((n_rows, share), BF16),
            jax.ShapeDtypeStruct((cut * heads, lanes), BF16),
        ),
        in_specs=[pl.BlockSpec(memory_space=pltpu.MemorySpace.HBM)] * 9,
        out_specs=(vmem, vmem),
        scratch_shapes=[pltpu.VMEM(a.shape, a.dtype) for a in operands]
        + [
            pltpu.VMEM((width, lanes), BF16),
            pltpu.VMEM((width, lanes), BF16),
            pltpu.VMEM((2, n_rows, lanes), BF16),
            pltpu.VMEM((2, n_rows, lanes), BF16),
            pltpu.VMEM((n_mp, block, lanes), BF16),
            pltpu.VMEM((n_mp, n_rows, lanes), BF16),
            pltpu.VMEM((n_dp, n_rows, cut), BF16),
            pltpu.VMEM((n_dp, n_rows, cut), BF16),
            pltpu.VMEM((n_rows, 2 * lanes), BF16),
            pltpu.VMEM((n_dp, n_rows, 2 * lanes), BF16),
            pltpu.VMEM((n_mp, n_rows, block), BF16),
            pltpu.VMEM((n_mp, n_rows, share), BF16),
            pltpu.VMEM((n_mp, n_rows, share), BF16),
            pltpu.VMEM((n_mp, n_rows, share), BF16),
            pltpu.VMEM((n_mp, n_rows, share), BF16),
            pltpu.VMEM((lanes, cut), BF16),
            pltpu.VMEM((lanes, cut), BF16),
            sems(2, n_dp),
            sems(2, n_dp),
            sems(2, n_dp),
            sems(2, n_mp),
            sems(2, n_mp),
            sems(2, pieces, n_mp),
            sems(2, pieces, n_mp),
            sems(2, pieces, n_mp),
            sems(2, pieces, n_mp),
            sems(2),
            sems(2),
            sems(n_mp),
            sems(8),
            sems(2),
        ],
        compiler_params=pltpu.CompilerParams(
            collective_id=0, has_side_effects=True, vmem_limit_bytes=67043328
        ),
    )(*operands)
    layer_out, grads = pl.pallas_call(
        hand_over,
        out_shape=(
            jax.ShapeDtypeStruct(layer_out.shape, BF16),
            jax.ShapeDtypeStruct(grads.shape, BF16),
        ),
        in_specs=[vmem] * 2,
        out_specs=(vmem, vmem),
        compiler_params=pltpu.CompilerParams(vmem_limit_bytes=67043328),
    )(layer_out, grads)
    return (layer_out, grads.reshape(1, cut, heads, lanes))


def solution(mesh):
    in_specs = (
        P("sec", "dp", None),
        P("sec", None, "mp", None),
        P("dp", None),
        P(),
        P(None, None, ("sec", "mp")),
        P(("sec", "mp"), None),
        P(("sec", "mp")),
        P("dp", None),
        P("dp", None),
    )
    out_specs = (P("dp", ("sec", "mp")), P("sec", "dp", "mp", None))
    return jax.shard_map(
        functools.partial(on_device, mesh.shape["dp"], mesh.shape["mp"]),
        mesh=mesh,
        in_specs=in_specs,
        out_specs=out_specs,
        check_vma=False,
    )
```

profile of v0, /device:TPU:1, one launch (start us, length us, event | category | flops | bytes accessed | tf_op | source)
XLA Modules:
  0.0 47.5 jit_solution(14132652410489192387)
XLA Ops:
  0.6 44.9 %shard_map.104 = (bf16[128,512]{1,0:T(8,128)(2,1)}, bf16[2048,128]{1,0:T(8,128)(2,1)}) custom-call(bf16[128,4096]{1,0:T(8,128)(2,1)} %bitcast.10, bf16[8192,128]{1,0:T(8,128)(2,1)} %bitcast.9, bf16[128,4096]{1,0:T(8,128)(2,1)} %grad_hbm.1, f32[1,4096]{1,0:T(1,128)} %bitcast.11, bf16[384,4096]{1,0:T(8,128)(2,1)} %bitcast.8, bf16[192,4096]{1,0:T(8,128)(2,1)} %ffn_out_hbm.1, ...), custom_call_target="tpu_custom_call" | custom-call | tf_op jit(solution)/shard_map/pallas_call | solution.py:493
  45.5 2.0 %shard_map.105 = (bf16[128,512]{1,0:T(8,128)(2,1)}, bf16[2048,128]{1,0:T(8,128)(2,1)}) custom-call(bf16[128,512]{1,0:T(8,128)(2,1)} %get-tuple-element.6.a, bf16[2048,128]{1,0:T(8,128)(2,1)} %get-tuple-element.7.b), custom_call_target="tpu_custom_call" | custom-call | tf_op jit(solution)/shard_map/pallas_call | solution.py:539
where the time goes:
time: 48 us; the launch traced here: 47.5 us
  Pallas kernels  46.9 us (98%)
  between operations  0.64 us (1%)
    pallas_call x1, Pallas kernels, on_device(): pl.pallas_call(functools.partial(body, n_dp, n_mp), out_shape=(jax.ShapeD...  44.9 us
    pallas_call x1, Pallas kernels, on_device(): pl.pallas_call(hand_over, out_shape=(jax.ShapeDtypeStruct(layer_out.shape...  1.96 us

commit v1 on v0

v1 whole, which is shorter than its diff:
```python
import functools
import math

import jax
import jax.numpy as jnp
from jax import lax
from jax.experimental import pallas as pl
from jax.experimental.pallas import tpu as pltpu
from jax.sharding import PartitionSpec as P

norm_eps = 1e-06
pieces = 2
most_relays = 4
F32 = jnp.float32
BF16 = jnp.bfloat16


def contract(left, right, left_dim, right_dim):
    dims = (((left_dim,), (right_dim,)), ((), ()))
    return lax.dot_general(left, right, dims, preferred_element_type=F32)


def remote(src, dst, send, recv, device):
    return pltpu.make_async_remote_copy(
        src_ref=src,
        dst_ref=dst,
        send_sem=send,
        recv_sem=recv,
        device_id=device,
        device_id_type=pl.DeviceIdType.MESH,
    )


def body(
    n_dp,
    n_mp,
    rows_hbm,
    weight_hbm,
    grad_hbm,
    gain_hbm,
    ffn_in_hbm,
    ffn_out_hbm,
    level_hbm,
    dec_seg_hbm,
    enc_seg_hbm,
    layer_out,
    proj_grads,
    rows,
    weight,
    grad,
    gain,
    ffn_in,
    level,
    dec_seg,
    enc_seg,
    down_own,
    down_other,
    w_left,
    w_right,
    kv_send,
    kv_recv,
    wo_all,
    ctx_all,
    rows_all,
    grad_all,
    g_send,
    g_all,
    mix,
    gate_up,
    square,
    hid_own,
    hid_other,
    partial,
    fold_send,
    fold_recv,
    t_left,
    t_right,
    rows_sem,
    grad_sem,
    g_sem,
    wo_sem,
    relay_sem,
    ctx_sem,
    mix_send,
    mix_recv,
    fwd_sem,
    hid_sem,
    fold_sem,
    fold_got,
    kv_sem,
    gkv_sem,
    down_sem,
    weight_sem,
    load_sem,
    slot_sem,
):
    sec = lax.axis_index("sec")
    dp = lax.axis_index("dp")
    mp = lax.axis_index("mp")
    n_rows, width = rows.shape
    lanes = weight.shape[1]
    half = lanes // 2
    block = width // n_mp
    share = width // (2 * n_mp)
    cut = width // n_dp
    units = down_own.shape[0]
    hubs = n_mp == 4
    if hubs:
        hub = mp * (3 - mp) // 2
        mate = mp + 1 - 2 * lax.rem(mp, 2)
        far_hub = 3 - mp * hub - mate * (1 - hub)
        far_end = 3 - mate * hub - mp * (1 - hub)
        arrivals = [mate, far_hub, far_end]
        targets = [mate, 2 - mp // 2]
        is_hub = hub == 1
    else:
        arrivals = [lax.rem(mp + n_mp - t, n_mp) for t in range(1, n_mp)]
        targets = [lax.rem(mp + t, n_mp) for t in range(1, n_mp)]
    piece_rows = n_rows // pieces
    relays = math.gcd(n_dp, most_relays)
    part = block // relays
    turn = lax.rem(dp, relays)
    is_dec = sec == 1
    is_enc = sec == 0
    other = {"sec": 1 - sec}

    def dp_at(t):
        return lax.rem(dp + t, n_dp)

    def mp_at(t):
        return lax.rem(mp + t, n_mp)

    def turn_at(s):
        return lax.rem(turn + s, relays)

    def cols(index, size):
        return pl.ds(pl.multiple_of(index * size, size), size)

    def piece(c):
        return pl.ds(c * piece_rows, piece_rows)

    def signal(device):
        pl.semaphore_signal(barrier, inc=1, device_id=device, device_id_type=pl.DeviceIdType.MESH)

    def weight_load(t):
        where = cols(mp_at(t), 2 * block)
        return pltpu.make_async_copy(
            weight_hbm.at[where, :], weight.at[where, :], weight_sem.at[t]
        )

    pairs = (
        (rows_hbm, rows),
        (grad_hbm, grad),
        (dec_seg_hbm, dec_seg),
        (enc_seg_hbm, enc_seg),
        (gain_hbm, gain),
        (level_hbm, level),
        (ffn_in_hbm, ffn_in),
        (ffn_out_hbm.at[:, cols(sec, width // 2)], down_own),
    )
    loads = [pltpu.make_async_copy(a, b, load_sem.at[i]) for i, (a, b) in enumerate(pairs)]
    own_rows = pltpu.make_async_copy(rows_hbm.at[:, cols(dp, cut)], rows_all.at[0], slot_sem.at[0])
    own_grad = pltpu.make_async_copy(grad_hbm.at[:, cols(dp, cut)], grad_all.at[0], slot_sem.at[1])

    def rows_copy(t):
        to = dp_at(t)
        return remote(
            rows_hbm.at[:, cols(to, cut)], rows_all.at[t], rows_sem.at[0, t], rows_sem.at[1, t], {"dp": to}
        )

    def grad_copy(t):
        to = dp_at(t)
        return remote(
            grad_hbm.at[:, cols(to, cut)], grad_all.at[t], grad_sem.at[0, t], grad_sem.at[1, t], {"dp": to}
        )

    def g_copy(t):
        return remote(
            g_all.at[0], g_all.at[t], g_sem.at[0, t], g_sem.at[1, t], {"dp": dp_at(t)}
        )

    def slot(t):
        return slice(t * lanes, (t + 1) * lanes)

    def adjacent(t, sending):
        if t == 1:
            return mp < n_mp - 1 if sending else mp > 0
        return mp > 0 if sending else mp < n_mp - 1

    def near_far(t, sending, near, far):
        if 1 < t < n_mp - 1:
            far()
        else:
            pl.when(adjacent(t, sending))(near)
            pl.when(jnp.logical_not(adjacent(t, sending)))(far)

    def wo_copy(t):
        to = mp_at(t)
        return remote(
            w_right.at[cols(to * relays + turn, part), :],
            wo_all.at[cols(turn, part), slot(t)],
            wo_sem.at[0, t],
            wo_sem.at[1, t],
            {"mp": to},
        )

    def wo_whole(t):
        to = mp_at(t)
        return remote(
            w_right.at[cols(to, block), :],
            wo_all.at[:, slot(t)],
            wo_sem.at[0, t],
            wo_sem.at[1, t],
            {"mp": to},
        )

    def relay_out(t, s):
        ref = wo_all.at[cols(turn, part), slot(t)]
        to = {"dp": dp - turn + turn_at(s)}
        return remote(ref, ref, relay_sem.at[0, t, s], relay_sem.at[1, t, s], to)

    def relay_in(t, s):
        ref = wo_all.at[cols(turn_at(relays - s), part), slot(t)]
        to = {"dp": dp - turn + turn_at(s)}
        return remote(ref, ref, relay_sem.at[0, t, s], relay_sem.at[1, t, s], to)

    def ctx_copy(t):
        return remote(
            ctx_all.at[:, slot(0)],
            ctx_all.at[:, slot(t)],
            ctx_sem.at[0, t],
            ctx_sem.at[1, t],
            {"mp": mp_at(t)},
        )

    def mix_copy(c, b, j):
        ref = mix.at[b, piece(c), :]
        return remote(ref, ref, mix_send.at[j, c, b], mix_recv.at[c, b], {"mp": targets[j]})

    def fwd_copy(c, b):
        ref = mix.at[b, piece(c), :]
        return remote(ref, ref, fwd_sem.at[0, c, b], fwd_sem.at[1, c, b], other)

    def hid_copy(c):
        return remote(
            hid_own.at[piece(c), :], hid_other.at[piece(c), :], hid_sem.at[0, c], hid_sem.at[1, c], other
        )

    def fold_copy(c, k):
        if hubs:
            into = 1 + (1 - hub) * k if k else 0
            to = hub * arrivals[k] + (1 - hub) * mate
        else:
            into, to = k, arrivals[k]
        return remote(
            fold_send.at[k, piece(c), :],
            fold_recv.at[into, piece(c), :],
            fold_sem.at[c, k],
            fold_got.at[c, into],
            {"mp": to},
        )

    def fold_in(c, k):
        return remote(
            fold_send.at[0, piece(c), :],
            fold_recv.at[k, piece(c), :],
            fold_sem.at[c, 0],
            fold_got.at[c, k],
            {"mp": arrivals[0]},
        )

    kv_copy = remote(kv_send, kv_recv, kv_sem.at[0], kv_sem.at[1], other)
    gkv_copy = remote(g_send, g_all.at[0], gkv_sem.at[0], gkv_sem.at[1], other)
    down_copy = remote(
        ffn_out_hbm.at[:, cols(1 - sec, width // 2)], down_other, down_sem.at[0], down_sem.at[1], other
    )

    with jax.named_scope("signals"):
        barrier = pltpu.get_barrier_semaphore()
        for t in list(range(1, n_mp)) + [0]:
            weight_load(t).start()
        for load in loads[:1]:
            load.start()
        signal(other)
        for t in range(1, n_dp):
            signal({"dp": dp_at(t)})
        for t in range(1, n_mp):
            signal({"mp": mp_at(t)})
        for load in loads[1:6]:
            load.start()

    tile = 2 * lanes
    out_id = lax.broadcasted_iota(jnp.int32, (tile, tile), 0)
    in_id = lax.broadcasted_iota(jnp.int32, (tile, tile), 1)
    wanted = jnp.where(out_id < lanes, 2 * out_id, 2 * (out_id - lanes) + 1)
    pick = jnp.where(in_id == wanted, 1.0, 0.0).astype(BF16)
    first = lax.broadcasted_iota(jnp.int32, (lanes, lanes), 1) < half

    with jax.named_scope("split"):
        for t in list(range(1, n_mp)) + [0]:
            begin = mp_at(t) * block
            weight_load(t).wait()
            for i in range(block // lanes):
                d = pl.multiple_of(begin + i * lanes, lanes)
                two = contract(pick, weight[pl.ds(pl.multiple_of(2 * d, tile), tile), :], 1, 0)
                one, second = two[:lanes], two[lanes:]
                w_left[pl.ds(d, lanes), :] = jnp.where(
                    first, one, pltpu.roll(second, half, 1)
                ).astype(BF16)
                w_right[pl.ds(d, lanes), :] = jnp.where(
                    first, pltpu.roll(one, half, 1), second
                ).astype(BF16)

    with jax.named_scope("barrier"):
        pl.semaphore_wait(barrier, n_dp + n_mp - 1)

    @pl.when(is_dec)
    def _():
        with jax.named_scope("wo_start"):
            for whole in range(2):
                for t in range(1, n_mp):
                    near_far(
                        t,
                        True,
                        (lambda: wo_whole(t).start()) if whole else (lambda: None),
                        (lambda: None) if whole else (lambda: wo_copy(t).start()),
                    )

    loads[0].wait()

    @pl.when(is_enc)
    def _():
        with jax.named_scope("kv"):
            kv_send[0] = contract(rows[...], w_left[...], 1, 0).astype(BF16)
            kv_send[1] = contract(rows[...], w_right[...], 1, 0).astype(BF16)
            kv_copy.start()
            rows_copy(1).start()

    for load in loads[6:]:
        load.start()
    own_rows.start()
    down_copy.start()
    for load in loads[1:6]:
        load.wait()

    @pl.when(is_dec)
    def _():
        own_grad.start()
        with jax.named_scope("q_gc"):
            wide_q = contract(rows[...], w_left[...], 1, 0)
            wide_gc = contract(grad[...], w_right[...], 1, 0)
            q = wide_q.astype(BF16)
            gc = wide_gc.astype(BF16)
            dec = jnp.transpose(jnp.broadcast_to(dec_seg[...].astype(F32), (n_rows, n_rows)))
            same = dec == jnp.broadcast_to(enc_seg[...].astype(F32), (n_rows, n_rows))
            wo_all[:, slot(0)] = w_right[cols(mp, block), :]
        with jax.named_scope("relay"):
            for t in range(1, n_mp):

                def pass_quarter():
                    wo_copy(t).wait_recv()
                    for s in range(1, relays):
                        relay_out(t, s).start()

                near_far(t, False, lambda: None, pass_quarter)
        with jax.named_scope("kv_wait"):
            kv_copy.wait_recv()
        with jax.named_scope("attend"):
            key = kv_recv[0]
            value = kv_recv[1]
            probs, lows, contexts = [], [], []
            for h in range(2):
                mine = first if h == 0 else jnp.logical_not(first)
                scores = contract(jnp.where(mine, wide_q, 0.0).astype(BF16), key, 1, 1)
                scores = jnp.where(same, scores, -1e30)
                scores = jnp.exp(scores - jnp.max(scores, axis=1, keepdims=True))
                prob = scores / jnp.sum(scores, axis=1, keepdims=True)
                low = prob.astype(BF16)
                probs.append(prob)
                lows.append(low)
                contexts.append(contract(low, value, 1, 0))
            context = jnp.where(first, contexts[0], contexts[1]).astype(BF16)
            ctx_all[:, slot(0)] = context
            g_all[0, :, lanes:] = context
            for t in range(1, n_mp):
                ctx_copy(t).start()
        with jax.named_scope("attend_back"):
            gqs, gks, gvs = [], [], []
            for h in range(2):
                mine = first if h == 0 else jnp.logical_not(first)
                grad_prob = contract(jnp.where(mine, wide_gc, 0.0).astype(BF16), value, 1, 1)
                total = jnp.sum(grad_prob * probs[h], axis=1, keepdims=True)
                score = (probs[h] * (grad_prob - total)).astype(BF16)
                gqs.append(contract(score, key, 1, 0))
                gks.append(contract(score, q, 0, 0))
                gvs.append(contract(lows[h], gc, 0, 0))
            g_send[:, :lanes] = jnp.where(first, gks[0], gks[1]).astype(BF16)
            g_send[:, lanes:] = jnp.where(first, gvs[0], gvs[1]).astype(BF16)
            gkv_copy.start()
            g_all[0, :, :lanes] = jnp.where(first, gqs[0], gqs[1]).astype(BF16)

    @pl.when(is_enc)
    def _():
        with jax.named_scope("gkv_wait"):
            gkv_copy.wait_recv()
            for t in range(2, n_dp):
                rows_copy(t).start()

    for t in range(1, n_dp):
        g_copy(t).start()

    @pl.when(is_dec)
    def _():
        with jax.named_scope("wo_wait"):
            for t in range(1, n_mp):

                def take_quarters():
                    for s in range(1, relays):
                        relay_in(t, s).wait_recv()

                near_far(t, False, lambda: wo_whole(t).wait_recv(), take_quarters)
        for t in range(1, n_dp):
            rows_copy(t).start()
            grad_copy(t).start()
        with jax.named_scope("ctx_wait"):
            for t in range(1, n_mp):
                ctx_copy(t).wait_recv()
        with jax.named_scope("mix"):
            for c in range(pieces):
                own = contract(ctx_all[piece(c), :], wo_all[...], 1, 1)
                total = rows[piece(c), cols(mp, block)].astype(F32) + own
                mix[mp, piece(c), :] = total.astype(BF16)

                for j in range(len(targets)):
                    mix_copy(c, mp, j).start()
                fwd_copy(c, mp).start()

    for load in loads[6:]:
        load.wait()

    def take(c, b, fresh):
        where = cols(b, block)
        wide = mix[b, piece(c), :].astype(F32)
        scaled = (wide * gain[:, where]).astype(BF16)
        both = contract(scaled, ffn_in[:, where], 1, 1)
        squares = jnp.broadcast_to(jnp.sum(wide * wide, axis=1, keepdims=True), (piece_rows, lanes))
        if fresh:
            gate_up[piece(c), :] = both
            square[piece(c), :] = squares
        else:
            gate_up[piece(c), :] += both
            square[piece(c), :] += squares

    place = sec * n_mp + mp
    with jax.named_scope("own_mix"):
        for c in range(pieces):

            @pl.when(is_enc)
            def _():
                fwd_copy(c, mp).wait_recv()

            take(c, mp, True)

    def gather(c):
        for k, b in enumerate(arrivals):

            @pl.when(is_dec)
            def _():
                mix_copy(c, b, 0).wait_recv()
                if hubs and k > 0:

                    @pl.when(is_hub)
                    def _():
                        mix_copy(c, b, 0).start()

                fwd_copy(c, b).start()

            @pl.when(is_enc)
            def _():
                fwd_copy(c, b).wait_recv()

            take(c, b, False)

    def finish(c):
        with jax.named_scope("hidden%d" % c):
            inverse = lax.rsqrt(square[piece(c), :1] / width + norm_eps)
            gate = gate_up[piece(c), :units] * inverse
            up = gate_up[piece(c), units:] * inverse
            unit_level = level[...].astype(F32) * 0.25
            hidden = (jax.nn.gelu(gate, approximate=True) * up * unit_level).astype(BF16)
            hid_own[piece(c), :] = hidden
            hid_copy(c).start()
            if c == 0:
                down_copy.wait_recv()
            hid_copy(c).wait_recv()
        with jax.named_scope("down%d" % c):

            def product(b):
                where = cols(b, share)
                own = contract(hidden, down_own[:, where], 1, 0)
                return own + contract(hid_other[piece(c), :], down_other[:, where], 1, 0)

            for k in reversed(range(n_mp - 1)):
                own = product(arrivals[k])
                fold_send[k, piece(c), :] = own.astype(BF16)
                if not hubs or k == 0:
                    fold_copy(c, k).start()
                else:
                    partial[k, piece(c), :] = own

                    @pl.when(jnp.logical_not(is_hub))
                    def _():
                        fold_copy(c, k).start()

            there = cols(lax.rem(place, 2), share)
            partial[0, piece(c), :] = product(mp) + mix[place // 2, piece(c), there].astype(F32)

    def combine(c):
        if hubs:

            @pl.when(is_hub)
            def _():
                for k in range(n_mp - 2, 0, -1):
                    fold_in(c, k + 1).wait_recv()
                    total = partial[k, piece(c), :] + fold_recv[k + 1, piece(c), :].astype(F32)
                    fold_send[k, piece(c), :] = total.astype(BF16)
                    fold_copy(c, k).start()

    for c in range(pieces):
        with jax.named_scope("gather%d" % c):
            gather(c)
        finish(c)
        if c:
            with jax.named_scope("combine%d" % (c - 1)):
                combine(c - 1)
    with jax.named_scope("combine%d" % (pieces - 1)):
        combine(pieces - 1)

    own_rows.wait()

    @pl.when(is_dec)
    def _():
        own_grad.wait()

    with jax.named_scope("dp_wait"):
        for t in range(1, n_dp):
            rows_copy(t).wait_recv()

            @pl.when(is_dec)
            def _():
                grad_copy(t).wait_recv()

            g_copy(t).wait_recv()
    with jax.named_scope("weight_grads"):
        flat_rows = rows_all[...].reshape(n_dp * n_rows, cut)
        g_flat = g_all[...].reshape(n_dp * n_rows, 2 * lanes)
        t_left[...] = contract(g_flat[:, :lanes], flat_rows, 0, 0).astype(BF16)

        @pl.when(is_enc)
        def _():
            t_right[...] = contract(g_flat[:, lanes:], flat_rows, 0, 0).astype(BF16)

        @pl.when(is_dec)
        def _():
            flat_grad = grad_all[...].reshape(n_dp * n_rows, cut)
            t_right[...] = contract(g_flat[:, lanes:], flat_grad, 0, 0).astype(BF16)

        row_id = lax.broadcasted_iota(jnp.int32, (tile, lanes), 0)
        d_id = lax.broadcasted_iota(jnp.int32, (tile, lanes), 1)
        spread = [jnp.where(row_id == 2 * d_id + h, 1.0, 0.0).astype(BF16) for h in range(2)]
        for i in range(cut // lanes):
            some = slice(i * lanes, (i + 1) * lanes)
            heads = [
                jnp.concatenate(
                    [t_left[h * half : (h + 1) * half, some], t_right[h * half : (h + 1) * half, some]],
                    axis=0,
                )
                for h in range(2)
            ]
            woven = contract(spread[0], heads[0], 1, 1) + contract(spread[1], heads[1], 1, 1)
            proj_grads[i * tile : (i + 1) * tile, :] = woven.astype(BF16)

    with jax.named_scope("fold"):
        for c in range(pieces):
            mine = partial[0, piece(c), :]
            for k in range(2 if hubs else n_mp - 1):
                fold_in(c, k).wait_recv()
                mine = mine + fold_recv[k, piece(c), :].astype(F32)
            layer_out[piece(c), :] = mine.astype(BF16)

    with jax.named_scope("drain"):
        down_copy.wait_send()
        for t in range(1, n_dp):
            rows_copy(t).wait_send()
            g_copy(t).wait_send()
        for c in range(pieces):
            hid_copy(c).wait_send()
            for k in range(n_mp - 1):
                fold_copy(c, k).wait_send()

        @pl.when(is_enc)
        def _():
            kv_copy.wait_send()

        @pl.when(is_dec)
        def _():
            gkv_copy.wait_send()
            for t in range(1, n_dp):
                grad_copy(t).wait_send()
            for t in range(1, n_mp):
                near_far(t, True, lambda: wo_whole(t).wait_send(), lambda: wo_copy(t).wait_send())
                ctx_copy(t).wait_send()

                def sent_quarters():
                    for s in range(1, relays):
                        relay_out(t, s).wait_send()

                near_far(t, False, lambda: None, sent_quarters)
            for c in range(pieces):
                fwd_copy(c, mp).wait_send()
                for j in range(len(targets)):
                    mix_copy(c, mp, j).wait_send()
                for k, b in enumerate(arrivals):
                    fwd_copy(c, b).wait_send()
                    if hubs and k > 0:

                        @pl.when(is_hub)
                        def _():
                            mix_copy(c, b, 0).wait_send()


def hand_over(a, b, a_out, b_out):
    a_out[...] = a[...]
    b_out[...] = b[...]


def on_device(
    n_dp,
    n_mp,
    section_rows,
    proj_weights,
    out_grad,
    ffn_gain,
    ffn_in,
    ffn_out,
    grow_level,
    dec_seg,
    enc_seg,
):
    rows = section_rows[0]
    n_rows, width = rows.shape
    heads, lanes = proj_weights.shape[2:]
    weight = proj_weights.reshape(width * heads, lanes)
    units = ffn_out.shape[0]
    gates = jnp.transpose(ffn_in, (1, 2, 0)).reshape(2 * units, width)
    block, share, cut = width // n_mp, width // (2 * n_mp), width // n_dp
    relays = math.gcd(n_dp, most_relays)
    vmem = pl.BlockSpec(memory_space=pltpu.VMEM)

    def sems(*shape):
        return pltpu.SemaphoreType.DMA(shape)

    operands = (
        rows,
        weight,
        out_grad,
        ffn_gain[None],
        gates,
        ffn_out,
        grow_level[None],
        dec_seg,
        enc_seg,
    )
    layer_out, grads = pl.pallas_call(
        functools.partial(body, n_dp, n_mp),
        out_shape=(
            jax.ShapeDtypeStruct((n_rows, share), BF16),
            jax.ShapeDtypeStruct((cut * heads, lanes), BF16),
        ),
        in_specs=[pl.BlockSpec(memory_space=pltpu.MemorySpace.HBM)] * 9,
        out_specs=(vmem, vmem),
        scratch_shapes=[pltpu.VMEM(a.shape, a.dtype) for a in operands if a is not ffn_out]
        + [
            pltpu.VMEM((units, width // 2), BF16),
            pltpu.VMEM((units, width // 2), BF16),
            pltpu.VMEM((width, lanes), BF16),
            pltpu.VMEM((width, lanes), BF16),
            pltpu.VMEM((2, n_rows, lanes), BF16),
            pltpu.VMEM((2, n_rows, lanes), BF16),
            pltpu.VMEM((block, n_mp * lanes), BF16),
            pltpu.VMEM((n_rows, n_mp * lanes), BF16),
            pltpu.VMEM((n_dp, n_rows, cut), BF16),
            pltpu.VMEM((n_dp, n_rows, cut), BF16),
            pltpu.VMEM((n_rows, 2 * lanes), BF16),
            pltpu.VMEM((n_dp, n_rows, 2 * lanes), BF16),
            pltpu.VMEM((n_mp, n_rows, block), BF16),
            pltpu.VMEM((n_rows, 2 * units), F32),
            pltpu.VMEM((n_rows, lanes), F32),
            pltpu.VMEM((n_rows, units), BF16),
            pltpu.VMEM((n_rows, units), BF16),
            pltpu.VMEM((n_mp, n_rows, share), F32),
            pltpu.VMEM((n_mp, n_rows, share), BF16),
            pltpu.VMEM((n_mp, n_rows, share), BF16),
            pltpu.VMEM((lanes, cut), BF16),
            pltpu.VMEM((lanes, cut), BF16),
            sems(2, n_dp),
            sems(2, n_dp),
            sems(2, n_dp),
            sems(2, n_mp),
            sems(2, n_mp, relays),
            sems(2, n_mp),
            sems(n_mp, pieces, n_mp),
            sems(pieces, n_mp),
            sems(2, pieces, n_mp),
            sems(2, pieces),
            sems(pieces, n_mp),
            sems(pieces, n_mp),
            sems(2),
            sems(2),
            sems(2),
            sems(n_mp),
            sems(8),
            sems(2),
        ],
        compiler_params=pltpu.CompilerParams(
            collective_id=0, has_side_effects=True, vmem_limit_bytes=67043328
        ),
    )(*operands)
    layer_out, grads = pl.pallas_call(
        hand_over,
        out_shape=(
            jax.ShapeDtypeStruct(layer_out.shape, BF16),
            jax.ShapeDtypeStruct(grads.shape, BF16),
        ),
        in_specs=[vmem] * 2,
        out_specs=(vmem, vmem),
        compiler_params=pltpu.CompilerParams(vmem_limit_bytes=67043328),
    )(layer_out, grads)
    return (layer_out, grads.reshape(1, cut, heads, lanes))


def solution(mesh):
    in_specs = (
        P("sec", "dp", None),
        P("sec", None, "mp", None),
        P("dp", None),
        P(),
        P(None, None, ("sec", "mp")),
        P(("sec", "mp"), None),
        P(("sec", "mp")),
        P("dp", None),
        P("dp", None),
    )
    out_specs = (P("dp", ("sec", "mp")), P("sec", "dp", "mp", None))
    return jax.shard_map(
        functools.partial(on_device, mesh.shape["dp"], mesh.shape["mp"]),
        mesh=mesh,
        in_specs=in_specs,
        out_specs=out_specs,
        check_vma=False,
    )
```

time: 48 us -> 46.1 us (0.960)
  Pallas kernels: 46.9 us -> 45 us
    pallas_call x1, Pallas kernels: 44.9 us -> 43 us  [on_device(): pl.pallas_call(functools.partial(body, n_dp, n_mp), out_shape=(jax.ShapeD...]
where the time goes in v1:
time: 46.1 us; the launch traced here: 45.7 us
  Pallas kernels  45 us (98%)
  between operations  0.64 us (1%)
    pallas_call x1, Pallas kernels, on_device(): pl.pallas_call(functools.partial(body, n_dp, n_mp), out_shape=(jax.ShapeD...  43 us
    pallas_call x1, Pallas kernels, on_device(): pl.pallas_call(hand_over, out_shape=(jax.ShapeDtypeStruct(layer_out.shape...  1.96 us

profile of v1, /device:TPU:1, one launch (start us, length us, event | category | flops | bytes accessed | tf_op | source)
XLA Modules:
  0.0 45.7 jit_solution(3410907779877785014)
XLA Ops:
  0.6 43.0 %shard_map.104 = (bf16[128,512]{1,0:T(8,128)(2,1)}, bf16[2048,128]{1,0:T(8,128)(2,1)}) custom-call(bf16[128,4096]{1,0:T(8,128)(2,1)} %bitcast.10, bf16[8192,128]{1,0:T(8,128)(2,1)} %bitcast.9, bf16[128,4096]{1,0:T(8,128)(2,1)} %grad_hbm.1, f32[1,4096]{1,0:T(1,128)} %bitcast.11, bf16[384,4096]{1,0:T(8,128)(2,1)} %bitcast.8, bf16[192,4096]{1,0:T(8,128)(2,1)} %ffn_out_hbm.1, ...), custom_call_target="tpu_custom_call" | custom-call | tf_op jit(solution)/shard_map/pallas_call | solution.py:674
  43.7 2.0 %shard_map.105 = (bf16[128,512]{1,0:T(8,128)(2,1)}, bf16[2048,128]{1,0:T(8,128)(2,1)}) custom-call(bf16[128,512]{1,0:T(8,128)(2,1)} %get-tuple-element.6.a, bf16[2048,128]{1,0:T(8,128)(2,1)} %get-tuple-element.7.b), custom_call_target="tpu_custom_call" | custom-call | tf_op jit(solution)/shard_map/pallas_call | solution.py:729

commit v2 on v1

--- a/solution.py
+++ b/solution.py
@@ -9,7 +9,12 @@
 from jax.sharding import PartitionSpec as P
 
 norm_eps = 1e-06
-pieces = 2
+eighths = (4, 4)
+eager = True
+piped = False
+fold_hubs = True
+mix_hubs = False
+pieces = len(eighths)
 most_relays = 4
 F32 = jnp.float32
 BF16 = jnp.bfloat16
@@ -104,19 +109,29 @@
     share = width // (2 * n_mp)
     cut = width // n_dp
     units = down_own.shape[0]
-    hubs = n_mp == 4
-    if hubs:
+    hubs = n_mp == 4 and fold_hubs
+    passing = n_mp == 4 and mix_hubs
+    if n_mp == 4:
         hub = mp * (3 - mp) // 2
         mate = mp + 1 - 2 * lax.rem(mp, 2)
         far_hub = 3 - mp * hub - mate * (1 - hub)
         far_end = 3 - mate * hub - mp * (1 - hub)
+        is_hub = hub == 1
+    if hubs:
         arrivals = [mate, far_hub, far_end]
-        targets = [mate, 2 - mp // 2]
-        is_hub = hub == 1
     else:
         arrivals = [lax.rem(mp + n_mp - t, n_mp) for t in range(1, n_mp)]
+    if passing:
+        targets = [mate, 2 - mp // 2]
+        sequence = [
+            hub * far_hub + (1 - hub) * mate,
+            hub * far_end + (1 - hub) * far_hub,
+            hub * mate + (1 - hub) * far_end,
+        ]
+    else:
         targets = [lax.rem(mp + t, n_mp) for t in range(1, n_mp)]
-    piece_rows = n_rows // pieces
+        sequence = [lax.rem(mp + n_mp - t, n_mp) for t in range(1, n_mp)]
+    starts = [sum(eighths[:c]) * n_rows // 8 for c in range(pieces + 1)]
     relays = math.gcd(n_dp, most_relays)
     part = block // relays
     turn = lax.rem(dp, relays)
@@ -137,7 +152,7 @@
         return pl.ds(pl.multiple_of(index * size, size), size)
 
     def piece(c):
-        return pl.ds(c * piece_rows, piece_rows)
+        return pl.ds(starts[c], starts[c + 1] - starts[c])
 
     def signal(device):
         pl.semaphore_signal(barrier, inc=1, device_id=device, device_id_type=pl.DeviceIdType.MESH)
@@ -269,15 +284,20 @@
             {"mp": arrivals[0]},
         )
 
+    def send_own(c):
+        for j in range(len(targets)):
+            mix_copy(c, mp, j).start()
+
     kv_copy = remote(kv_send, kv_recv, kv_sem.at[0], kv_sem.at[1], other)
     gkv_copy = remote(g_send, g_all.at[0], gkv_sem.at[0], gkv_sem.at[1], other)
     down_copy = remote(
         ffn_out_hbm.at[:, cols(1 - sec, width // 2)], down_other, down_sem.at[0], down_sem.at[1], other
     )
 
+    order = list(range(2, n_mp - 1)) + [1, n_mp - 1, 0]
     with jax.named_scope("signals"):
         barrier = pltpu.get_barrier_semaphore()
-        for t in list(range(1, n_mp)) + [0]:
+        for t in order:
             weight_load(t).start()
         for load in loads[:1]:
             load.start()
@@ -286,8 +306,6 @@
             signal({"dp": dp_at(t)})
         for t in range(1, n_mp):
             signal({"mp": mp_at(t)})
-        for load in loads[1:6]:
-            load.start()
 
     tile = 2 * lanes
     out_id = lax.broadcasted_iota(jnp.int32, (tile, tile), 0)
@@ -296,8 +314,8 @@
     pick = jnp.where(in_id == wanted, 1.0, 0.0).astype(BF16)
     first = lax.broadcasted_iota(jnp.int32, (lanes, lanes), 1) < half
 
-    with jax.named_scope("split"):
-        for t in list(range(1, n_mp)) + [0]:
+    for t in order:
+        with jax.named_scope("split%d" % t):
             begin = mp_at(t) * block
             weight_load(t).wait()
             for i in range(block // lanes):
@@ -310,21 +328,16 @@
                 w_right[pl.ds(d, lanes), :] = jnp.where(
                     first, pltpu.roll(one, half, 1), second
                 ).astype(BF16)
-
-    with jax.named_scope("barrier"):
-        pl.semaphore_wait(barrier, n_dp + n_mp - 1)
-
-    @pl.when(is_dec)
-    def _():
-        with jax.named_scope("wo_start"):
-            for whole in range(2):
-                for t in range(1, n_mp):
-                    near_far(
-                        t,
-                        True,
-                        (lambda: wo_whole(t).start()) if whole else (lambda: None),
-                        (lambda: None) if whole else (lambda: wo_copy(t).start()),
-                    )
+        if t == order[0]:
+            for load in loads[1:6]:
+                load.start()
+            with jax.named_scope("barrier"):
+                pl.semaphore_wait(barrier, n_dp + n_mp - 1)
+        if t > 0:
+
+            @pl.when(is_dec)
+            def _():
+                near_far(t, True, lambda: None, lambda: wo_copy(t).start())
 
     loads[0].wait()
 
@@ -334,7 +347,6 @@
             kv_send[0] = contract(rows[...], w_left[...], 1, 0).astype(BF16)
             kv_send[1] = contract(rows[...], w_right[...], 1, 0).astype(BF16)
             kv_copy.start()
-            rows_copy(1).start()
 
     for load in loads[6:]:
         load.start()
@@ -363,6 +375,8 @@
                         relay_out(t, s).start()
 
                 near_far(t, False, lambda: None, pass_quarter)
+            for t in (1, n_mp - 1):
+                near_far(t, True, lambda: wo_whole(t).start(), lambda: None)
         with jax.named_scope("kv_wait"):
             kv_copy.wait_recv()
         with jax.named_scope("attend"):
@@ -403,11 +417,6 @@
     def _():
         with jax.named_scope("gkv_wait"):
             gkv_copy.wait_recv()
-            for t in range(2, n_dp):
-                rows_copy(t).start()
-
-    for t in range(1, n_dp):
-        g_copy(t).start()
 
     @pl.when(is_dec)
     def _():
@@ -422,6 +431,7 @@
         for t in range(1, n_dp):
             rows_copy(t).start()
             grad_copy(t).start()
+            g_copy(t).start()
         with jax.named_scope("ctx_wait"):
             for t in range(1, n_mp):
                 ctx_copy(t).wait_recv()
@@ -431,8 +441,8 @@
                 total = rows[piece(c), cols(mp, block)].astype(F32) + own
                 mix[mp, piece(c), :] = total.astype(BF16)
 
-                for j in range(len(targets)):
-                    mix_copy(c, mp, j).start()
+                if c == 0 or eager:
+                    send_own(c)
                 fwd_copy(c, mp).start()
 
     for load in loads[6:]:
@@ -443,7 +453,8 @@
         wide = mix[b, piece(c), :].astype(F32)
         scaled = (wide * gain[:, where]).astype(BF16)
         both = contract(scaled, ffn_in[:, where], 1, 1)
-        squares = jnp.broadcast_to(jnp.sum(wide * wide, axis=1, keepdims=True), (piece_rows, lanes))
+        squares = jnp.sum(wide * wide, axis=1, keepdims=True)
+        squares = jnp.broadcast_to(squares, (wide.shape[0], lanes))
         if fresh:
             gate_up[piece(c), :] = both
             square[piece(c), :] = squares
@@ -452,28 +463,30 @@
             square[piece(c), :] += squares
 
     place = sec * n_mp + mp
-    with jax.named_scope("own_mix"):
-        for c in range(pieces):
-
-            @pl.when(is_enc)
-            def _():
-                fwd_copy(c, mp).wait_recv()
-
-            take(c, mp, True)
-
     def gather(c):
-        for k, b in enumerate(arrivals):
+        @pl.when(is_enc)
+        def _():
+            fwd_copy(c, mp).wait_recv()
+            if c == 0:
+                for t in range(1, n_dp):
+                    rows_copy(t).start()
+                    g_copy(t).start()
+
+        take(c, mp, True)
+        for k, b in enumerate(sequence):
 
             @pl.when(is_dec)
             def _():
                 mix_copy(c, b, 0).wait_recv()
-                if hubs and k > 0:
+                if passing and k < 2:
 
                     @pl.when(is_hub)
                     def _():
                         mix_copy(c, b, 0).start()
 
                 fwd_copy(c, b).start()
+                if not eager and c + 1 < pieces and k == min(1, len(arrivals) - 1):
+                    send_own(c + 1)
 
             @pl.when(is_enc)
             def _():
@@ -481,7 +494,7 @@
 
             take(c, b, False)
 
-    def finish(c):
+    def activate(c):
         with jax.named_scope("hidden%d" % c):
             inverse = lax.rsqrt(square[piece(c), :1] / width + norm_eps)
             gate = gate_up[piece(c), :units] * inverse
@@ -490,10 +503,14 @@
             hidden = (jax.nn.gelu(gate, approximate=True) * up * unit_level).astype(BF16)
             hid_own[piece(c), :] = hidden
             hid_copy(c).start()
+
+    def descend(c):
+        with jax.named_scope("hid_wait%d" % c):
             if c == 0:
                 down_copy.wait_recv()
             hid_copy(c).wait_recv()
         with jax.named_scope("down%d" % c):
+            hidden = hid_own[piece(c), :]
 
             def product(b):
                 where = cols(b, share)
@@ -529,12 +546,19 @@
     for c in range(pieces):
         with jax.named_scope("gather%d" % c):
             gather(c)
-        finish(c)
-        if c:
-            with jax.named_scope("combine%d" % (c - 1)):
-                combine(c - 1)
-    with jax.named_scope("combine%d" % (pieces - 1)):
-        combine(pieces - 1)
+        activate(c)
+        if piped and c > 0:
+            descend(c - 1)
+        if not piped:
+            descend(c)
+        if c > 1:
+            with jax.named_scope("combine%d" % (c - 2)):
+                combine(c - 2)
+    if piped:
+        descend(pieces - 1)
+    for c in range(max(pieces - 2, 0), pieces):
+        with jax.named_scope("combine%d" % c):
+            combine(c)
 
     own_rows.wait()
 
@@ -620,18 +644,21 @@
                 fwd_copy(c, mp).wait_send()
                 for j in range(len(targets)):
                     mix_copy(c, mp, j).wait_send()
-                for k, b in enumerate(arrivals):
+                for k, b in enumerate(sequence):
                     fwd_copy(c, b).wait_send()
-                    if hubs and k > 0:
+                    if passing and k < 2:
 
                         @pl.when(is_hub)
                         def _():
                             mix_copy(c, b, 0).wait_send()
 
 
-def hand_over(a, b, a_out, b_out):
-    a_out[...] = a[...]
-    b_out[...] = b[...]
+def hand_over(a, b, a_out, b_out, sem):
+    copies = [pltpu.make_async_copy(a, a_out, sem.at[0]), pltpu.make_async_copy(b, b_out, sem.at[1])]
+    for copy in copies:
+        copy.start()
+    for copy in copies:
+        copy.wait()
 
 
 def on_device(
@@ -674,8 +701,8 @@
     layer_out, grads = pl.pallas_call(
         functools.partial(body, n_dp, n_mp),
         out_shape=(
-            jax.ShapeDtypeStruct((n_rows, share), BF16),
-            jax.ShapeDtypeStruct((cut * heads, lanes), BF16),
+            pltpu.VMEM((n_rows, share), BF16),
+            pltpu.VMEM((cut * heads, lanes), BF16),
         ),
         in_specs=[pl.BlockSpec(memory_space=pltpu.MemorySpace.HBM)] * 9,
         out_specs=(vmem, vmem),
@@ -723,7 +750,7 @@
             sems(2),
         ],
         compiler_params=pltpu.CompilerParams(
-            collective_id=0, has_side_effects=True, vmem_limit_bytes=67043328
+            collective_id=0, has_side_effects=True, vmem_limit_bytes=58 << 20
         ),
     )(*operands)
     layer_out, grads = pl.pallas_call(
@@ -733,9 +760,9 @@
             jax.ShapeDtypeStruct(grads.shape, BF16),
         ),
         in_specs=[vmem] * 2,
-        out_specs=(vmem, vmem),
-        compiler_params=pltpu.CompilerParams(vmem_limit_bytes=67043328),
-    )(layer_out, grads)
+        out_specs=(pl.BlockSpec(memory_space=pl.ANY),) * 2,
+        scratch_shapes=[pltpu.SemaphoreType.DMA((2,))],
+    )(*(pltpu.with_memory_space_constraint(a, pltpu.VMEM) for a in (layer_out, grads)))
     return (layer_out, grads.reshape(1, cut, heads, lanes))
 
 

time: 46.1 us -> 41.3 us (0.90)
  Pallas kernels: 45 us -> 40.2 us
    pallas_call x1, Pallas kernels: 43 us -> 39.3 us  [on_device(): pl.pallas_call(functools.partial(body, n_dp, n_mp), out_shape=(pltpu.VMEM...]
    pallas_call x1, Pallas kernels: 1.96 us -> 0.86 us  [on_device(): pl.pallas_call(hand_over, out_shape=(jax.ShapeDtypeStruct(layer_out.shape...]
where the time goes in v2:
time: 41.3 us; the launch traced here: 40.8 us
  Pallas kernels  40.2 us (97%)
  between operations  0.64 us (2%)
    pallas_call x1, Pallas kernels, on_device(): pl.pallas_call(functools.partial(body, n_dp, n_mp), out_shape=(pltpu.VMEM...  39.3 us
    pallas_call x1, Pallas kernels, on_device(): pl.pallas_call(hand_over, out_shape=(jax.ShapeDtypeStruct(layer_out.shape...  0.86 us

profile of v2, /device:TPU:1, one launch (start us, length us, event | category | flops | bytes accessed | tf_op | source)
XLA Modules:
  0.0 40.8 jit_solution(2893185628703974325)
XLA Ops:
  0.6 39.3 %shard_map.104 = (bf16[128,512]{1,0:T(8,128)(2,1)S(1)}, bf16[2048,128]{1,0:T(8,128)(2,1)S(1)}) custom-call(bf16[128,4096]{1,0:T(8,128)(2,1)} %bitcast.10, bf16[8192,128]{1,0:T(8,128)(2,1)} %bitcast.9, bf16[128,4096]{1,0:T(8,128)(2,1)} %grad_hbm.1, f32[1,4096]{1,0:T(1,128)} %bitcast.11, bf16[384,4096]{1,0:T(8,128)(2,1)} %bitcast.8, ...), custom_call_target="tpu_custom_call" | custom-call | tf_op jit(solution)/shard_map/pallas_call | solution.py:701
  40.0 0.9 %shard_map.105 = (bf16[128,512]{1,0:T(8,128)(2,1)}, bf16[2048,128]{1,0:T(8,128)(2,1)}) custom-call(bf16[128,512]{1,0:T(8,128)(2,1)S(1)} %get-tuple-element.6.a, bf16[2048,128]{1,0:T(8,128)(2,1)S(1)} %get-tuple-element.7.b), custom_call_target="tpu_custom_call" | custom-call | tf_op jit(solution)/shard_map/pallas_call | solution.py:756

commit v3 on v2

--- a/solution.py
+++ b/solution.py
@@ -128,6 +128,9 @@
             hub * far_end + (1 - hub) * far_hub,
             hub * mate + (1 - hub) * far_end,
         ]
+    elif n_mp == 4:
+        targets = [far_end, far_hub, mate]
+        sequence = [mate, far_hub, far_end]
     else:
         targets = [lax.rem(mp + t, n_mp) for t in range(1, n_mp)]
         sequence = [lax.rem(mp + n_mp - t, n_mp) for t in range(1, n_mp)]
@@ -180,18 +183,18 @@
     def rows_copy(t):
         to = dp_at(t)
         return remote(
-            rows_hbm.at[:, cols(to, cut)], rows_all.at[t], rows_sem.at[0, t], rows_sem.at[1, t], {"dp": to}
+            rows_hbm.at[:, cols(to, cut)], rows_all.at[t], rows_sem.at[0, t - 1], rows_sem.at[1, t - 1], {"dp": to}
         )
 
     def grad_copy(t):
         to = dp_at(t)
         return remote(
-            grad_hbm.at[:, cols(to, cut)], grad_all.at[t], grad_sem.at[0, t], grad_sem.at[1, t], {"dp": to}
+            grad_hbm.at[:, cols(to, cut)], grad_all.at[t], grad_sem.at[0, t - 1], grad_sem.at[1, t - 1], {"dp": to}
         )
 
     def g_copy(t):
         return remote(
-            g_all.at[0], g_all.at[t], g_sem.at[0, t], g_sem.at[1, t], {"dp": dp_at(t)}
+            g_all.at[0], g_all.at[t], g_sem.at[0, t - 1], g_sem.at[1, t - 1], {"dp": dp_at(t)}
         )
 
     def slot(t):
@@ -214,8 +217,8 @@
         return remote(
             w_right.at[cols(to * relays + turn, part), :],
             wo_all.at[cols(turn, part), slot(t)],
-            wo_sem.at[0, t],
-            wo_sem.at[1, t],
+            wo_sem.at[0, t - 1],
+            wo_sem.at[1, t - 1],
             {"mp": to},
         )
 
@@ -224,33 +227,33 @@
         return remote(
             w_right.at[cols(to, block), :],
             wo_all.at[:, slot(t)],
-            wo_sem.at[0, t],
-            wo_sem.at[1, t],
+            wo_sem.at[0, t - 1],
+            wo_sem.at[1, t - 1],
             {"mp": to},
         )
 
     def relay_out(t, s):
         ref = wo_all.at[cols(turn, part), slot(t)]
         to = {"dp": dp - turn + turn_at(s)}
-        return remote(ref, ref, relay_sem.at[0, t, s], relay_sem.at[1, t, s], to)
+        return remote(ref, ref, relay_sem.at[0, t - 1, s - 1], relay_sem.at[1, t - 1, s - 1], to)
 
     def relay_in(t, s):
         ref = wo_all.at[cols(turn_at(relays - s), part), slot(t)]
         to = {"dp": dp - turn + turn_at(s)}
-        return remote(ref, ref, relay_sem.at[0, t, s], relay_sem.at[1, t, s], to)
+        return remote(ref, ref, relay_sem.at[0, t - 1, s - 1], relay_sem.at[1, t - 1, s - 1], to)
 
     def ctx_copy(t):
         return remote(
             ctx_all.at[:, slot(0)],
             ctx_all.at[:, slot(t)],
-            ctx_sem.at[0, t],
-            ctx_sem.at[1, t],
+            ctx_sem.at[0, t - 1],
+            ctx_sem.at[1, t - 1],
             {"mp": mp_at(t)},
         )
 
     def mix_copy(c, b, j):
         ref = mix.at[b, piece(c), :]
-        return remote(ref, ref, mix_send.at[j, c, b], mix_recv.at[c, b], {"mp": targets[j]})
+        return remote(ref, ref, mix_send.at[j, c], mix_recv.at[c, b], {"mp": targets[j]})
 
     def fwd_copy(c, b):
         ref = mix.at[b, piece(c), :]
@@ -295,6 +298,11 @@
     )
 
     order = list(range(2, n_mp - 1)) + [1, n_mp - 1, 0]
+    if n_dp == 4:
+        beside = 1 + 2 * lax.rem(dp, 2)
+        near_dp, far_dp = [beside, 2], [4 - beside]
+    else:
+        near_dp, far_dp = [1], list(range(2, n_dp))
     with jax.named_scope("signals"):
         barrier = pltpu.get_barrier_semaphore()
         for t in order:
@@ -333,6 +341,12 @@
                 load.start()
             with jax.named_scope("barrier"):
                 pl.semaphore_wait(barrier, n_dp + n_mp - 1)
+
+            @pl.when(is_enc)
+            def _():
+                for t in near_dp:
+                    rows_copy(t).start()
+
         if t > 0:
 
             @pl.when(is_dec)
@@ -358,6 +372,8 @@
     @pl.when(is_dec)
     def _():
         own_grad.start()
+        for t in (1, n_mp - 1):
+            near_far(t, True, lambda: wo_whole(t).start(), lambda: None)
         with jax.named_scope("q_gc"):
             wide_q = contract(rows[...], w_left[...], 1, 0)
             wide_gc = contract(grad[...], w_right[...], 1, 0)
@@ -367,7 +383,7 @@
             same = dec == jnp.broadcast_to(enc_seg[...].astype(F32), (n_rows, n_rows))
             wo_all[:, slot(0)] = w_right[cols(mp, block), :]
         with jax.named_scope("relay"):
-            for t in range(1, n_mp):
+            for t in order[:-1]:
 
                 def pass_quarter():
                     wo_copy(t).wait_recv()
@@ -375,8 +391,6 @@
                         relay_out(t, s).start()
 
                 near_far(t, False, lambda: None, pass_quarter)
-            for t in (1, n_mp - 1):
-                near_far(t, True, lambda: wo_whole(t).start(), lambda: None)
         with jax.named_scope("kv_wait"):
             kv_copy.wait_recv()
         with jax.named_scope("attend"):
@@ -468,8 +482,9 @@
         def _():
             fwd_copy(c, mp).wait_recv()
             if c == 0:
+                for t in far_dp:
+                    rows_copy(t).start()
                 for t in range(1, n_dp):
-                    rows_copy(t).start()
                     g_copy(t).start()
 
         take(c, mp, True)
@@ -505,20 +520,25 @@
             hid_copy(c).start()
 
     def descend(c):
+        with jax.named_scope("down_own%d" % c):
+            hidden = hid_own[piece(c), :]
+            for k in reversed(range(n_mp - 1)):
+                partial[k, piece(c), :] = contract(hidden, down_own[:, cols(arrivals[k], share)], 1, 0)
         with jax.named_scope("hid_wait%d" % c):
             if c == 0:
                 down_copy.wait_recv()
             hid_copy(c).wait_recv()
         with jax.named_scope("down%d" % c):
-            hidden = hid_own[piece(c), :]
+            beside_hidden = hid_other[piece(c), :]
 
             def product(b):
                 where = cols(b, share)
                 own = contract(hidden, down_own[:, where], 1, 0)
-                return own + contract(hid_other[piece(c), :], down_other[:, where], 1, 0)
+                return own + contract(beside_hidden, down_other[:, where], 1, 0)
 
             for k in reversed(range(n_mp - 1)):
-                own = product(arrivals[k])
+                other_part = contract(beside_hidden, down_other[:, cols(arrivals[k], share)], 1, 0)
+                own = partial[k, piece(c), :] + other_part
                 fold_send[k, piece(c), :] = own.astype(BF16)
                 if not hubs or k == 0:
                     fold_copy(c, k).start()
@@ -730,13 +750,13 @@
             pltpu.VMEM((n_mp, n_rows, share), BF16),
             pltpu.VMEM((lanes, cut), BF16),
             pltpu.VMEM((lanes, cut), BF16),
-            sems(2, n_dp),
-            sems(2, n_dp),
-            sems(2, n_dp),
+            sems(2, n_dp - 1),
+            sems(2, n_dp - 1),
+            sems(2, n_dp - 1),
+            sems(2, n_mp - 1),
+            sems(2, n_mp - 1, max(relays - 1, 1)),
             sems(2, n_mp),
-            sems(2, n_mp, relays),
-            sems(2, n_mp),
-            sems(n_mp, pieces, n_mp),
+            sems(n_mp - 1, pieces),
             sems(pieces, n_mp),
             sems(2, pieces, n_mp),
             sems(2, pieces),

time: 41.3 us -> 39.5 us (0.956)
  Pallas kernels: 40.2 us -> 38.3 us
    pallas_call x1, Pallas kernels: 39.3 us -> 37.4 us  [on_device(): pl.pallas_call(functools.partial(body, n_dp, n_mp), out_shape=(pltpu.VMEM...]
where the time goes in v3:
time: 39.5 us; the launch traced here: 38.9 us
  Pallas kernels  38.3 us (97%)
  between operations  0.64 us (2%)
    pallas_call x1, Pallas kernels, on_device(): pl.pallas_call(functools.partial(body, n_dp, n_mp), out_shape=(pltpu.VMEM...  37.4 us
    pallas_call x1, Pallas kernels, on_device(): pl.pallas_call(hand_over, out_shape=(jax.ShapeDtypeStruct(layer_out.shape...  0.86 us

profile of v3, /device:TPU:1, one launch (start us, length us, event | category | flops | bytes accessed | tf_op | source)
XLA Modules:
  0.0 38.9 jit_solution(14665743805952397379)
XLA Ops:
  0.6 37.4 %shard_map.104 = (bf16[128,512]{1,0:T(8,128)(2,1)S(1)}, bf16[2048,128]{1,0:T(8,128)(2,1)S(1)}) custom-call(bf16[128,4096]{1,0:T(8,128)(2,1)} %bitcast.10, bf16[8192,128]{1,0:T(8,128)(2,1)} %bitcast.9, bf16[128,4096]{1,0:T(8,128)(2,1)} %grad_hbm.1, f32[1,4096]{1,0:T(1,128)} %bitcast.11, bf16[384,4096]{1,0:T(8,128)(2,1)} %bitcast.8, ...), custom_call_target="tpu_custom_call" | custom-call | tf_op jit(solution)/shard_map/pallas_call | solution.py:721
  38.1 0.9 %shard_map.105 = (bf16[128,512]{1,0:T(8,128)(2,1)}, bf16[2048,128]{1,0:T(8,128)(2,1)}) custom-call(bf16[128,512]{1,0:T(8,128)(2,1)S(1)} %get-tuple-element.6.a, bf16[2048,128]{1,0:T(8,128)(2,1)S(1)} %get-tuple-element.7.b), custom_call_target="tpu_custom_call" | custom-call | tf_op jit(solution)/shard_map/pallas_call | solution.py:776

commit v4 on v3

--- a/solution.py
+++ b/solution.py
@@ -10,10 +10,6 @@
 
 norm_eps = 1e-06
 eighths = (4, 4)
-eager = True
-piped = False
-fold_hubs = True
-mix_hubs = False
 pieces = len(eighths)
 most_relays = 4
 F32 = jnp.float32
@@ -88,6 +84,7 @@
     ctx_sem,
     mix_send,
     mix_recv,
+    fwd_sent,
     fwd_sem,
     hid_sem,
     fold_sem,
@@ -109,9 +106,8 @@
     share = width // (2 * n_mp)
     cut = width // n_dp
     units = down_own.shape[0]
-    hubs = n_mp == 4 and fold_hubs
-    passing = n_mp == 4 and mix_hubs
-    if n_mp == 4:
+    hubs = n_mp == 4
+    if hubs:
         hub = mp * (3 - mp) // 2
         mate = mp + 1 - 2 * lax.rem(mp, 2)
         far_hub = 3 - mp * hub - mate * (1 - hub)
@@ -121,14 +117,7 @@
         arrivals = [mate, far_hub, far_end]
     else:
         arrivals = [lax.rem(mp + n_mp - t, n_mp) for t in range(1, n_mp)]
-    if passing:
-        targets = [mate, 2 - mp // 2]
-        sequence = [
-            hub * far_hub + (1 - hub) * mate,
-            hub * far_end + (1 - hub) * far_hub,
-            hub * mate + (1 - hub) * far_end,
-        ]
-    elif n_mp == 4:
+    if n_mp == 4:
         targets = [far_end, far_hub, mate]
         sequence = [mate, far_hub, far_end]
     else:
@@ -183,19 +172,40 @@
     def rows_copy(t):
         to = dp_at(t)
         return remote(
-            rows_hbm.at[:, cols(to, cut)], rows_all.at[t], rows_sem.at[0, t - 1], rows_sem.at[1, t - 1], {"dp": to}
+            rows_hbm.at[:, cols(to, cut)], rows_all.at[t], rows_sem.at[0], rows_sem.at[1], {"dp": to}
         )
 
     def grad_copy(t):
         to = dp_at(t)
         return remote(
-            grad_hbm.at[:, cols(to, cut)], grad_all.at[t], grad_sem.at[0, t - 1], grad_sem.at[1, t - 1], {"dp": to}
+            grad_hbm.at[:, cols(to, cut)], grad_all.at[t], grad_sem.at[0], grad_sem.at[1], {"dp": to}
         )
 
     def g_copy(t):
         return remote(
-            g_all.at[0], g_all.at[t], g_sem.at[0, t - 1], g_sem.at[1, t - 1], {"dp": dp_at(t)}
-        )
+            g_all.at[0], g_all.at[t], g_sem.at[0], g_sem.at[1], {"dp": dp_at(t)}
+        )
+
+    def whole_of(ref, sem):
+        return remote(ref, ref, sem.at[0], sem.at[1], other)
+
+    peers = pl.ds(1, n_dp - 1)
+    rows_total = whole_of(rows_all.at[peers], rows_sem)
+    grad_total = whole_of(grad_all.at[peers], grad_sem)
+    g_total = whole_of(g_all.at[peers], g_sem)
+    ctx_total = whole_of(ctx_all.at[:, lanes:], ctx_sem)
+
+    def relay_total(t):
+        ref = wo_all.at[pl.ds(0, (relays - 1) * part), slot(t)]
+        return remote(ref, ref, relay_sem.at[0, t - 1], relay_sem.at[1, t - 1], other)
+
+    def mix_total(c, count, sem):
+        ref = mix.at[pl.ds(0, count), piece(c), :]
+        return remote(ref, ref, sem.at[c], mix_recv.at[c, 0], other)
+
+    def fold_total(c):
+        ref = fold_send.at[pl.ds(0, n_mp - 1), piece(c), :]
+        return remote(ref, ref, fold_sem.at[c], fold_got.at[c, 0], other)
 
     def slot(t):
         return slice(t * lanes, (t + 1) * lanes)
@@ -235,29 +245,29 @@
     def relay_out(t, s):
         ref = wo_all.at[cols(turn, part), slot(t)]
         to = {"dp": dp - turn + turn_at(s)}
-        return remote(ref, ref, relay_sem.at[0, t - 1, s - 1], relay_sem.at[1, t - 1, s - 1], to)
+        return remote(ref, ref, relay_sem.at[0, t - 1], relay_sem.at[1, t - 1], to)
 
     def relay_in(t, s):
         ref = wo_all.at[cols(turn_at(relays - s), part), slot(t)]
         to = {"dp": dp - turn + turn_at(s)}
-        return remote(ref, ref, relay_sem.at[0, t - 1, s - 1], relay_sem.at[1, t - 1, s - 1], to)
+        return remote(ref, ref, relay_sem.at[0, t - 1], relay_sem.at[1, t - 1], to)
 
     def ctx_copy(t):
         return remote(
             ctx_all.at[:, slot(0)],
             ctx_all.at[:, slot(t)],
-            ctx_sem.at[0, t - 1],
-            ctx_sem.at[1, t - 1],
+            ctx_sem.at[0],
+            ctx_sem.at[1],
             {"mp": mp_at(t)},
         )
 
     def mix_copy(c, b, j):
         ref = mix.at[b, piece(c), :]
-        return remote(ref, ref, mix_send.at[j, c], mix_recv.at[c, b], {"mp": targets[j]})
+        return remote(ref, ref, mix_send.at[c], mix_recv.at[c, b], {"mp": targets[j]})
 
     def fwd_copy(c, b):
         ref = mix.at[b, piece(c), :]
-        return remote(ref, ref, fwd_sem.at[0, c, b], fwd_sem.at[1, c, b], other)
+        return remote(ref, ref, fwd_sent.at[c], fwd_sem.at[c, b], other)
 
     def hid_copy(c):
         return remote(
@@ -273,7 +283,7 @@
         return remote(
             fold_send.at[k, piece(c), :],
             fold_recv.at[into, piece(c), :],
-            fold_sem.at[c, k],
+            fold_sem.at[c],
             fold_got.at[c, into],
             {"mp": to},
         )
@@ -282,7 +292,7 @@
         return remote(
             fold_send.at[0, piece(c), :],
             fold_recv.at[k, piece(c), :],
-            fold_sem.at[c, 0],
+            fold_sem.at[c],
             fold_got.at[c, k],
             {"mp": arrivals[0]},
         )
@@ -431,6 +441,8 @@
     def _():
         with jax.named_scope("gkv_wait"):
             gkv_copy.wait_recv()
+            for t in far_dp:
+                rows_copy(t).start()
 
     @pl.when(is_dec)
     def _():
@@ -438,8 +450,8 @@
             for t in range(1, n_mp):
 
                 def take_quarters():
-                    for s in range(1, relays):
-                        relay_in(t, s).wait_recv()
+                    if relays > 1:
+                        relay_total(t).wait_recv()
 
                 near_far(t, False, lambda: wo_whole(t).wait_recv(), take_quarters)
         for t in range(1, n_dp):
@@ -447,16 +459,14 @@
             grad_copy(t).start()
             g_copy(t).start()
         with jax.named_scope("ctx_wait"):
-            for t in range(1, n_mp):
-                ctx_copy(t).wait_recv()
+            ctx_total.wait_recv()
         with jax.named_scope("mix"):
             for c in range(pieces):
                 own = contract(ctx_all[piece(c), :], wo_all[...], 1, 1)
                 total = rows[piece(c), cols(mp, block)].astype(F32) + own
                 mix[mp, piece(c), :] = total.astype(BF16)
 
-                if c == 0 or eager:
-                    send_own(c)
+                send_own(c)
                 fwd_copy(c, mp).start()
 
     for load in loads[6:]:
@@ -482,8 +492,6 @@
         def _():
             fwd_copy(c, mp).wait_recv()
             if c == 0:
-                for t in far_dp:
-                    rows_copy(t).start()
                 for t in range(1, n_dp):
                     g_copy(t).start()
 
@@ -493,15 +501,7 @@
             @pl.when(is_dec)
             def _():
                 mix_copy(c, b, 0).wait_recv()
-                if passing and k < 2:
-
-                    @pl.when(is_hub)
-                    def _():
-                        mix_copy(c, b, 0).start()
-
                 fwd_copy(c, b).start()
-                if not eager and c + 1 < pieces and k == min(1, len(arrivals) - 1):
-                    send_own(c + 1)
 
             @pl.when(is_enc)
             def _():
@@ -524,6 +524,9 @@
             hidden = hid_own[piece(c), :]
             for k in reversed(range(n_mp - 1)):
                 partial[k, piece(c), :] = contract(hidden, down_own[:, cols(arrivals[k], share)], 1, 0)
+        if c > 0:
+            with jax.named_scope("combine%d" % (c - 1)):
+                combine(c - 1)
         with jax.named_scope("hid_wait%d" % c):
             if c == 0:
                 down_copy.wait_recv()
@@ -567,18 +570,9 @@
         with jax.named_scope("gather%d" % c):
             gather(c)
         activate(c)
-        if piped and c > 0:
-            descend(c - 1)
-        if not piped:
-            descend(c)
-        if c > 1:
-            with jax.named_scope("combine%d" % (c - 2)):
-                combine(c - 2)
-    if piped:
-        descend(pieces - 1)
-    for c in range(max(pieces - 2, 0), pieces):
-        with jax.named_scope("combine%d" % c):
-            combine(c)
+        descend(c)
+    with jax.named_scope("combine%d" % (pieces - 1)):
+        combine(pieces - 1)
 
     own_rows.wait()
 
@@ -587,14 +581,13 @@
         own_grad.wait()
 
     with jax.named_scope("dp_wait"):
-        for t in range(1, n_dp):
-            rows_copy(t).wait_recv()
-
-            @pl.when(is_dec)
-            def _():
-                grad_copy(t).wait_recv()
-
-            g_copy(t).wait_recv()
+        rows_total.wait_recv()
+        g_total.wait_recv()
+
+        @pl.when(is_dec)
+        def _():
+            grad_total.wait_recv()
+
     with jax.named_scope("weight_grads"):
         flat_rows = rows_all[...].reshape(n_dp * n_rows, cut)
         g_flat = g_all[...].reshape(n_dp * n_rows, 2 * lanes)
@@ -634,13 +627,11 @@
 
     with jax.named_scope("drain"):
         down_copy.wait_send()
-        for t in range(1, n_dp):
-            rows_copy(t).wait_send()
-            g_copy(t).wait_send()
+        rows_total.wait_send()
+        g_total.wait_send()
         for c in range(pieces):
             hid_copy(c).wait_send()
-            for k in range(n_mp - 1):
-                fold_copy(c, k).wait_send()
+            fold_total(c).wait_send()
 
         @pl.when(is_enc)
         def _():
@@ -649,28 +640,15 @@
         @pl.when(is_dec)
         def _():
             gkv_copy.wait_send()
-            for t in range(1, n_dp):
-                grad_copy(t).wait_send()
+            grad_total.wait_send()
+            ctx_total.wait_send()
             for t in range(1, n_mp):
                 near_far(t, True, lambda: wo_whole(t).wait_send(), lambda: wo_copy(t).wait_send())
-                ctx_copy(t).wait_send()
-
-                def sent_quarters():
-                    for s in range(1, relays):
-                        relay_out(t, s).wait_send()
-
-                near_far(t, False, lambda: None, sent_quarters)
+                if relays > 1:
+                    near_far(t, False, lambda: None, lambda: relay_total(t).wait_send())
             for c in range(pieces):
-                fwd_copy(c, mp).wait_send()
-                for j in range(len(targets)):
-                    mix_copy(c, mp, j).wait_send()
-                for k, b in enumerate(sequence):
-                    fwd_copy(c, b).wait_send()
-                    if passing and k < 2:
-
-                        @pl.when(is_hub)
-                        def _():
-                            mix_copy(c, b, 0).wait_send()
+                mix_total(c, n_mp, fwd_sent).wait_send()
+                mix_total(c, n_mp - 1, mix_send).wait_send()
 
 
 def hand_over(a, b, a_out, b_out, sem):
@@ -750,17 +728,18 @@
             pltpu.VMEM((n_mp, n_rows, share), BF16),
             pltpu.VMEM((lanes, cut), BF16),
             pltpu.VMEM((lanes, cut), BF16),
-            sems(2, n_dp - 1),
-            sems(2, n_dp - 1),
-            sems(2, n_dp - 1),
+            sems(2),
+            sems(2),
+            sems(2),
             sems(2, n_mp - 1),
-            sems(2, n_mp - 1, max(relays - 1, 1)),
-            sems(2, n_mp),
-            sems(n_mp - 1, pieces),
+            sems(2, n_mp - 1),
+            sems(2),
+            sems(pieces),
             sems(pieces, n_mp),
-            sems(2, pieces, n_mp),
+            sems(pieces),
+            sems(pieces, n_mp),
             sems(2, pieces),
-            sems(pieces, n_mp),
+            sems(pieces),
             sems(pieces, n_mp),
             sems(2),
             sems(2),

time: 39.5 us -> 37.7 us (0.954)
  Pallas kernels: 38.3 us -> 36.6 us
    pallas_call x1, Pallas kernels: 37.4 us -> 35.7 us  [on_device(): pl.pallas_call(functools.partial(body, n_dp, n_mp), out_shape=(pltpu.VMEM...]
where the time goes in v4:
time: 37.7 us; the launch traced here: 37.2 us
  Pallas kernels  36.6 us (97%)
  between operations  0.64 us (2%)
    pallas_call x1, Pallas kernels, on_device(): pl.pallas_call(functools.partial(body, n_dp, n_mp), out_shape=(pltpu.VMEM...  35.7 us
    pallas_call x1, Pallas kernels, on_device(): pl.pallas_call(hand_over, out_shape=(jax.ShapeDtypeStruct(layer_out.shape...  0.86 us

profile of v4, /device:TPU:1, one launch (start us, length us, event | category | flops | bytes accessed | tf_op | source)
XLA Modules:
  0.0 37.2 jit_solution(14237816631907939744)
XLA Ops:
  0.6 35.7 %shard_map.104 = (bf16[128,512]{1,0:T(8,128)(2,1)S(1)}, bf16[2048,128]{1,0:T(8,128)(2,1)S(1)}) custom-call(bf16[128,4096]{1,0:T(8,128)(2,1)} %bitcast.10, bf16[8192,128]{1,0:T(8,128)(2,1)} %bitcast.9, bf16[128,4096]{1,0:T(8,128)(2,1)} %grad_hbm.1, f32[1,4096]{1,0:T(1,128)} %bitcast.11, bf16[384,4096]{1,0:T(8,128)(2,1)} %bitcast.8, ...), custom_call_target="tpu_custom_call" | custom-call | tf_op jit(solution)/shard_map/pallas_call | solution.py:699
  36.4 0.9 %shard_map.105 = (bf16[128,512]{1,0:T(8,128)(2,1)}, bf16[2048,128]{1,0:T(8,128)(2,1)}) custom-call(bf16[128,512]{1,0:T(8,128)(2,1)S(1)} %get-tuple-element.6.a, bf16[2048,128]{1,0:T(8,128)(2,1)S(1)} %get-tuple-element.7.b), custom_call_target="tpu_custom_call" | custom-call | tf_op jit(solution)/shard_map/pallas_call | solution.py:755

commit v5 on v4

--- a/solution.py
+++ b/solution.py
@@ -118,7 +118,7 @@
     else:
         arrivals = [lax.rem(mp + n_mp - t, n_mp) for t in range(1, n_mp)]
     if n_mp == 4:
-        targets = [far_end, far_hub, mate]
+        targets = [far_end, mate, far_hub]
         sequence = [mate, far_hub, far_end]
     else:
         targets = [lax.rem(mp + t, n_mp) for t in range(1, n_mp)]
@@ -392,15 +392,6 @@
             dec = jnp.transpose(jnp.broadcast_to(dec_seg[...].astype(F32), (n_rows, n_rows)))
             same = dec == jnp.broadcast_to(enc_seg[...].astype(F32), (n_rows, n_rows))
             wo_all[:, slot(0)] = w_right[cols(mp, block), :]
-        with jax.named_scope("relay"):
-            for t in order[:-1]:
-
-                def pass_quarter():
-                    wo_copy(t).wait_recv()
-                    for s in range(1, relays):
-                        relay_out(t, s).start()
-
-                near_far(t, False, lambda: None, pass_quarter)
         with jax.named_scope("kv_wait"):
             kv_copy.wait_recv()
         with jax.named_scope("attend"):
@@ -422,6 +413,15 @@
             g_all[0, :, lanes:] = context
             for t in range(1, n_mp):
                 ctx_copy(t).start()
+        with jax.named_scope("relay"):
+            for t in order[:-1]:
+
+                def pass_quarter():
+                    wo_copy(t).wait_recv()
+                    for s in far_dp + near_dp if n_dp == relays else range(1, relays):
+                        relay_out(t, s).start()
+
+                near_far(t, False, lambda: None, pass_quarter)
         with jax.named_scope("attend_back"):
             gqs, gks, gvs = [], [], []
             for h in range(2):

time: 37.7 us -> 37.3 us (0.989)
  Pallas kernels: 36.6 us -> 36.2 us
where the time goes in v5:
time: 37.3 us; the launch traced here: 36.9 us
  Pallas kernels  36.2 us (97%)
  between operations  0.64 us (2%)
    pallas_call x1, Pallas kernels, on_device(): pl.pallas_call(functools.partial(body, n_dp, n_mp), out_shape=(pltpu.VMEM...  35.4 us
    pallas_call x1, Pallas kernels, on_device(): pl.pallas_call(hand_over, out_shape=(jax.ShapeDtypeStruct(layer_out.shape...  0.86 us

profile of v5, /device:TPU:1, one launch (start us, length us, event | category | flops | bytes accessed | tf_op | source)
XLA Modules:
  0.0 36.9 jit_solution(7047856878422323696)
XLA Ops:
  0.6 35.4 %shard_map.104 = (bf16[128,512]{1,0:T(8,128)(2,1)S(1)}, bf16[2048,128]{1,0:T(8,128)(2,1)S(1)}) custom-call(bf16[128,4096]{1,0:T(8,128)(2,1)} %bitcast.10, bf16[8192,128]{1,0:T(8,128)(2,1)} %bitcast.9, bf16[128,4096]{1,0:T(8,128)(2,1)} %grad_hbm.1, f32[1,4096]{1,0:T(1,128)} %bitcast.11, bf16[384,4096]{1,0:T(8,128)(2,1)} %bitcast.8, ...), custom_call_target="tpu_custom_call" | custom-call | tf_op jit(solution)/shard_map/pallas_call | solution.py:699
  36.0 0.9 %shard_map.105 = (bf16[128,512]{1,0:T(8,128)(2,1)}, bf16[2048,128]{1,0:T(8,128)(2,1)}) custom-call(bf16[128,512]{1,0:T(8,128)(2,1)S(1)} %get-tuple-element.6.a, bf16[2048,128]{1,0:T(8,128)(2,1)S(1)} %get-tuple-element.7.b), custom_call_target="tpu_custom_call" | custom-call | tf_op jit(solution)/shard_map/pallas_call | solution.py:755

commit v6 on v5

--- a/solution.py
+++ b/solution.py
@@ -119,7 +119,7 @@
         arrivals = [lax.rem(mp + n_mp - t, n_mp) for t in range(1, n_mp)]
     if n_mp == 4:
         targets = [far_end, mate, far_hub]
-        sequence = [mate, far_hub, far_end]
+        sequence = [mate, far_end, far_hub]
     else:
         targets = [lax.rem(mp + t, n_mp) for t in range(1, n_mp)]
         sequence = [lax.rem(mp + n_mp - t, n_mp) for t in range(1, n_mp)]

time: 37.3 us -> 37.2 us (level)
  no operation moved by 1% of the time
where the time goes in v6:
time: 37.2 us; the launch traced here: 37.1 us
  Pallas kernels  36.4 us (98%)
  between operations  0.64 us (2%)
    pallas_call x1, Pallas kernels, on_device(): pl.pallas_call(functools.partial(body, n_dp, n_mp), out_shape=(pltpu.VMEM...  35.6 us
    pallas_call x1, Pallas kernels, on_device(): pl.pallas_call(hand_over, out_shape=(jax.ShapeDtypeStruct(layer_out.shape...  0.86 us

profile of v6, /device:TPU:1, one launch (start us, length us, event | category | flops | bytes accessed | tf_op | source)
XLA Modules:
  0.0 37.1 jit_solution(8717231142894535013)
XLA Ops:
  0.6 35.6 %shard_map.104 = (bf16[128,512]{1,0:T(8,128)(2,1)S(1)}, bf16[2048,128]{1,0:T(8,128)(2,1)S(1)}) custom-call(bf16[128,4096]{1,0:T(8,128)(2,1)} %bitcast.10, bf16[8192,128]{1,0:T(8,128)(2,1)} %bitcast.9, bf16[128,4096]{1,0:T(8,128)(2,1)} %grad_hbm.1, f32[1,4096]{1,0:T(1,128)} %bitcast.11, bf16[384,4096]{1,0:T(8,128)(2,1)} %bitcast.8, ...), custom_call_target="tpu_custom_call" | custom-call | tf_op jit(solution)/shard_map/pallas_call | solution.py:699
  36.2 0.9 %shard_map.105 = (bf16[128,512]{1,0:T(8,128)(2,1)}, bf16[2048,128]{1,0:T(8,128)(2,1)}) custom-call(bf16[128,512]{1,0:T(8,128)(2,1)S(1)} %get-tuple-element.6.a, bf16[2048,128]{1,0:T(8,128)(2,1)S(1)} %get-tuple-element.7.b), custom_call_target="tpu_custom_call" | custom-call | tf_op jit(solution)/shard_map/pallas_call | solution.py:755
